TPU v7x, 32 devices: a whole 2x2x4 slice. The times are simulated.
32 devices in a mesh: ctx: 16 (over z, x, core), ch: 2 (over y).
Axes of the slice: x: 2, y: 2, z: 4, core: 2. Of those that a mesh axis runs over, the one named last changes fastest.
Arguments:
- q_proj: bfloat16 [512, 16384], P('ch', 'ctx'), may hold values from -6 to 6
- k_proj: bfloat16 [512, 16384], P('ch', 'ctx'), may hold values from -6 to 6
- v_proj: bfloat16 [512, 16384], P('ch', 'ctx'), may hold values from -6 to 6
- short_taps: bfloat16 [3, 512, 3], P(None, 'ch'), may hold values from -3.5 to 3.5
- long_filter: float32 [512, 16384], P('ch', 'ctx'), may hold values from -4 to 4
- skip_gain: float32 [512], P('ch'), may hold values from 0.5 to 1.5
- out_weight: bfloat16 [512, 4096], P(None, 'ch'), may hold values from -0.25 to 0.25
Outputs:
- block_out: bfloat16 [16384, 4096], P('ctx', 'ch')
All inputs are finite; a program needn't handle non-finite values.
Results may differ from a plain program's by a relative error of at most 0.012.
Values may be sent and summed in bfloat16 or wider, within the bound.
No kernel may reach another device: no remote copies, remote signals or barrier semaphores. Data moves between devices by JAX's collectives and lax.ppermute only.
A program may use at most 128 MiB of HBM per device.

v0:
```python
import math
import jax
import jax.numpy as jnp
from jax import lax
from jax.sharding import PartitionSpec as P

exact_mode = lax.Precision.HIGHEST


def passed_along(value, axis, steps):
    count = lax.axis_size(axis)
    initial, last = (max(0, -steps), min(count, count - steps))
    return lax.ppermute(value, axis, [(source, source + steps) for source in range(initial, last)])


def unit_table(numbers, modulus, direction):
    angle = (numbers % modulus).astype(jnp.float32) * (direction * 2.0 * math.pi / modulus)
    return (jnp.cos(angle), jnp.sin(angle))


def complex_contract(pattern, left_real, left_imag, right_real, right_imag):
    real_real = jnp.einsum(pattern, left_real, right_real, precision=exact_mode)
    imag_imag = jnp.einsum(pattern, left_imag, right_imag, precision=exact_mode)
    real_imag = jnp.einsum(pattern, left_real, right_imag, precision=exact_mode)
    imag_real = jnp.einsum(pattern, left_imag, right_real, precision=exact_mode)
    return (real_real - imag_imag, real_imag + imag_real)


def transform_last(real_part, imag_part, inverse):
    size_n = real_part.shape[-1]
    direction = 1.0 if inverse else -1.0
    factor = max([divisor for divisor in range(1, 129) if size_n % divisor == 0])
    if size_n <= 128 or factor == 1:
        counter = jnp.arange(size_n, dtype=jnp.int32)
        table_cos, table_sin = unit_table(counter[:, None] * counter[None, :], size_n, direction)
        return complex_contract("...a,ak->...k", real_part, imag_part, table_cos, table_sin)
    remain = size_n // factor
    leading = real_part.shape[:-1]
    outer = jnp.arange(factor, dtype=jnp.int32)
    inner = jnp.arange(remain, dtype=jnp.int32)
    table_cos, table_sin = unit_table(outer[:, None] * outer[None, :], factor, direction)
    section_real, section_imag = complex_contract(
        "...ab,ac->...cb",
        real_part.reshape(leading + (factor, remain)),
        imag_part.reshape(leading + (factor, remain)),
        table_cos,
        table_sin,
    )
    twist_cos, twist_sin = unit_table(outer[:, None] * inner[None, :], size_n, direction)
    section_real, section_imag = (
        section_real * twist_cos - section_imag * twist_sin,
        section_real * twist_sin + section_imag * twist_cos,
    )
    section_real, section_imag = transform_last(section_real, section_imag, inverse)
    return (
        jnp.swapaxes(section_real, -1, -2).reshape(leading + (size_n,)),
        jnp.swapaxes(section_imag, -1, -2).reshape(leading + (size_n,)),
    )


def short_filter(extended, weights, out_length):
    span = weights.shape[-1]
    summed = jnp.zeros(extended.shape[:-1] + (out_length,), jnp.float32)
    for offset in range(span):
        begin_at = span - 1 - offset
        summed = summed + weights[..., offset : offset + 1].astype(jnp.float32) * extended[
            ..., begin_at : begin_at + out_length
        ].astype(jnp.float32)
    return summed


def long_by_channel(signal, long_filter):
    moved_signal, moved_filter = (
        lax.all_to_all(signal, "ctx", split_axis=0, concat_axis=1, tiled=True),
        lax.all_to_all(long_filter, "ctx", split_axis=0, concat_axis=1, tiled=True),
    )
    seq_len = moved_signal.shape[1]
    both = jnp.stack([moved_signal, moved_filter])
    padded = jnp.concatenate([both, jnp.zeros_like(both)], axis=2)
    freq_real, freq_imag = transform_last(padded, jnp.zeros_like(padded), False)
    prod_real = freq_real[0] * freq_real[1] - freq_imag[0] * freq_imag[1]
    prod_imag = freq_real[0] * freq_imag[1] + freq_imag[0] * freq_real[1]
    time_real, time_imag = transform_last(prod_real, prod_imag, True)
    result_rows = time_real[:, :seq_len] * (1.0 / (2 * seq_len))
    return lax.all_to_all(result_rows, "ctx", split_axis=1, concat_axis=0, tiled=True)


def local(q_proj, k_proj, v_proj, short_taps, long_filter, skip_gain, out_weight):
    channels, tokens = q_proj.shape
    short_span = short_taps.shape[2]
    stacked = jnp.stack([q_proj, k_proj, v_proj])
    rim_short = passed_along(stacked[:, :, tokens - short_span + 1 :], "ctx", 1)
    filtered = short_filter(jnp.concatenate([rim_short, stacked], axis=2), short_taps, tokens)
    query_short = filtered[0]
    product_kv = (filtered[1] * filtered[2]).astype(jnp.bfloat16).astype(jnp.float32)
    long_out = long_by_channel(product_kv, long_filter)
    gated_rows = (query_short * (long_out + skip_gain[:, None] * product_kv)).astype(jnp.bfloat16)
    initial = jnp.zeros((tokens, out_weight.shape[1]), jnp.float32)
    piece = jax.tree.map(lambda part: lax.all_gather(part, "ch", axis=0, tiled=True), gated_rows)
    weight_rows = lax.slice_in_dim(out_weight, 0, piece.shape[0], axis=0)
    summed = initial + jnp.einsum(
        "cb,cd->bd", piece, weight_rows, preferred_element_type=jnp.float32
    )
    return summed.astype(jnp.bfloat16)


def solution(mesh):
    in_specs = (
        P("ch", "ctx"),
        P("ch", "ctx"),
        P("ch", "ctx"),
        P(None, "ch", None),
        P("ch", "ctx"),
        P("ch"),
        P(None, "ch"),
    )
    out_specs = P("ctx", "ch")
    return jax.shard_map(local, mesh=mesh, in_specs=in_specs, out_specs=out_specs, check_vma=False)
```

profile of v0, /device:TPU:0, one launch (start us, length us, event | category | flops | bytes accessed | tf_op | source)
XLA Modules:
  0.0 414.4 jit_solution(9834079985797515446)
XLA Ops:
  6.5 7.7 %all-to-all-start.1 = ((f32[16,16,1024]{2,1,0:T(8,128)}), f32[16,16,1024]{2,1,0:T(8,128)}, u32[]{:S(2)}, u32[]{:S(2)}) async-start(f32[16,16,1024]{2,1,0:T(8,128)} %bitcast.218), calls=%async_computation.1 | async-start | bytes 2097152 | tf_op jit(solution)/shard_map/all_to_all | solution.py:75
  25.2 12.0 %all-to-all-done.1 = f32[16,16,1024]{2,1,0:T(8,128)} async-done(((f32[16,16,1024]{2,1,0:T(8,128)}), f32[16,16,1024]{2,1,0:T(8,128)}, u32[]{:S(2)}, u32[]{:S(2)}) %all-to-all-start.1) | async-done | bytes 1048608 | tf_op jit(solution)/shard_map/all_to_all | solution.py:75
  37.2 14.4 %all-to-all-start = ((f32[16,16,1024]{2,1,0:T(8,128)}), f32[16,16,1024]{2,1,0:T(8,128)S(1)}, u32[]{:S(2)}, u32[]{:S(2)}) async-start(f32[16,16,1024]{2,1,0:T(8,128)} %bitcast.11), calls=%async_computation | async-start | bytes 2097152 | tf_op jit(solution)/shard_map/all_to_all | solution.py:74
  54.1 3.8 fusion.12
  57.8 3.8 fusion.10
  66.9 7.6 %all-to-all-done = f32[16,16,1024]{2,1,0:T(8,128)S(1)} async-done(((f32[16,16,1024]{2,1,0:T(8,128)}), f32[16,16,1024]{2,1,0:T(8,128)S(1)}, u32[]{:S(2)}, u32[]{:S(2)}) %all-to-all-start) | async-done | bytes 1048608 | tf_op jit(solution)/shard_map/all_to_all | solution.py:74
  81.2 4.7 %fusion.4 = f32[128,2,16,256]{3,0,2,1:T(8,128)S(1)} fusion(f32[128,2,16,256]{3,0,2,1:T(8,128)S(1)} %copy-done.10, f32[2,16,128,256]{3,2,1,0:T(8,128)S(1)} %bitcast.195), kind=kOutput, calls=%fused_computation.14 | convolution fusion | flops 1611890688 | bytes 12582912 | tf_op jit(solution)/shard_map/...ab,ac->...cb/dot_general | solution.py:22
  85.9 9.3 %add_bitcast_fusion.2 = (f32[2,16,128,256]{3,2,1,0:T(8,128)}, f32[2,16,128,256]{3,2,1,0:T(8,128)}) fusion(f32[128,2,16,256]{3,0,2,1:T(8,128)S(1)} %fusion.4, f32[128,256]{1,0:T(8,128)S(1)} %get-tuple-element.20, f32[128,256]{1,0:T(8,128)S(1)} %get-tuple-element.21, f32[128,2,16,256]{3,0,2,1:T(8,128)S(1)} %copy-done.11, f32[2,16,128,256]{3,2,1,0:T(8,128)S(1)} %bitcast.196), kind=kOutput, calls=%fused_computation.10 | convolution fusion | flops 1618182144 | bytes 21233664 | tf_op jit(solution)/shard_map/...ab,ac->...cb/dot_general | solution.py:24
  95.2 5.5 %copy.75 = f32[2,16,128,256]{2,1,3,0:T(8,128)} copy(f32[2,16,128,256]{3,2,1,0:T(8,128)} %get-tuple-element.6) | data formatting | bytes 8388608 | tf_op jit(solution)/shard_map/sub | solution.py:51
  100.7 5.4 %copy.76 = f32[2,16,128,128,2]{3,2,4,1,0:T(8,128)} copy(f32[2,16,128,128,2]{2,1,4,3,0:T(8,128)} %bitcast.200) | data formatting | bytes 8388608 | tf_op jit(solution)/shard_map/reshape | solution.py:44
  106.1 8.2 %fusion.37 = f32[128,2,16,128,2]{3,0,4,2,1:T(8,128)} fusion(f32[2,16,128,128,2]{3,2,4,1,0:T(8,128)} %copy.76), kind=kOutput, calls=%fused_computation.75 | convolution fusion | flops 1610842112 | bytes 8388608 | tf_op jit(solution)/shard_map/...ab,ac->...cb/dot_general | solution.py:24
  114.3 5.7 %fusion.35 = f32[128,2,16,128,2]{3,0,4,2,1:T(8,128)} fusion(f32[2,16,128,128,2]{3,2,4,1,0:T(8,128)S(1)} %copy-done.3), kind=kOutput, calls=%fused_computation.73 | convolution fusion | flops 1610842112 | bytes 8388608 | tf_op jit(solution)/shard_map/...ab,ac->...cb/dot_general | solution.py:22
  119.9 5.7 %copy.77 = f32[2,16,128,256]{2,1,3,0:T(8,128)} copy(f32[2,16,128,256]{3,2,1,0:T(8,128)} %get-tuple-element.5) | data formatting | bytes 8388608 | tf_op jit(solution)/shard_map/add | solution.py:52
  125.6 5.3 %copy.78 = f32[2,16,128,128,2]{3,2,4,1,0:T(8,128)} copy(f32[2,16,128,128,2]{2,1,4,3,0:T(8,128)} %bitcast.201) | data formatting | bytes 8388608 | tf_op jit(solution)/shard_map/reshape | solution.py:45
  130.9 7.8 %convolution_add_fusion = f32[128,2,16,128,2]{3,0,4,2,1:T(8,128)S(1)} fusion(f32[128,2,16,128,2]{3,0,4,2,1:T(8,128)} %fusion.37, f32[2,16,128,128,2]{3,2,4,1,0:T(8,128)} %copy.78), kind=kOutput, calls=%fused_computation.16 | convolution fusion | flops 1611890688 | bytes 12582912 | tf_op jit(solution)/shard_map/...ab,ac->...cb/dot_general | solution.py:25
  138.7 7.6 %add_bitcast_fusion.1 = (f32[2,16,128,128,2]{2,3,4,1,0:T(8,128)}, f32[2,16,128,128,2]{2,3,4,1,0:T(8,128)}) fusion(f32[128,2,16,128,2]{3,0,4,2,1:T(8,128)S(1)} %convolution_add_fusion, f32[128,2]{0,1:T(2,128)S(1)} %get-tuple-element.22, f32[128,2]{0,1:T(2,128)S(1)} %get-tuple-element.23, f32[128,2,16,128,2]{3,0,4,2,1:T(8,128)S(1)} %copy-done.12, ...), kind=kOutput, calls=%fused_computation.8 | convolution fusion | flops 1618182144 | bytes 20973568 | tf_op jit(solution)/shard_map/...ab,ac->...cb/dot_general | solution.py:23
  146.3 7.2 %copy.81 = f32[2,16,128,128,2]{3,4,2,1,0:T(2,128)} copy(f32[2,16,128,128,2]{2,3,4,1,0:T(8,128)} %get-tuple-element.8) | data formatting | bytes 8388608 | tf_op jit(solution)/shard_map/sub | solution.py:51
  153.5 18.1 %fusion.90 = f32[2,16,128,128,2]{3,4,2,1,0:T(2,128)} fusion(f32[2,16,128,128,2]{3,4,2,1,0:T(2,128)} %copy.81), kind=kOutput, calls=%fused_computation.128 | convolution fusion | flops 25165880 | bytes 8388608 | tf_op jit(solution)/shard_map/...a,ak->...k/dot_general | solution.py:22
  171.6 16.2 %fusion.92 = f32[2,16,128,128,2]{3,4,2,1,0:T(2,128)} fusion(f32[2,16,128,128,2]{3,4,2,1,0:T(2,128)S(1)} %copy-done.1), kind=kOutput, calls=%fused_computation.130 | convolution fusion | flops 25165880 | bytes 8388608 | tf_op jit(solution)/shard_map/...a,ak->...k/dot_general | solution.py:24
  187.8 7.2 %copy.82 = f32[2,16,128,128,2]{3,4,2,1,0:T(2,128)} copy(f32[2,16,128,128,2]{2,3,4,1,0:T(8,128)} %get-tuple-element.7) | data formatting | bytes 8388608 | tf_op jit(solution)/shard_map/add | solution.py:52
  195.1 18.5 %subtract_bitcast_fusion = f32[2,16,128,2,128]{4,3,2,1,0:T(2,128)} fusion(f32[2,16,128,128,2]{3,4,2,1,0:T(2,128)} %fusion.90, f32[2,16,128,128,2]{3,4,2,1,0:T(2,128)} %copy.82), kind=kOutput, calls=%fused_computation.7 | convolution fusion | flops 26214456 | bytes 12582912 | tf_op jit(solution)/shard_map/...a,ak->...k/dot_general | solution.py:23
  213.6 6.4 %reshape.226 = f32[2,16,128,256]{3,2,1,0:T(8,128)} reshape(f32[2,16,128,2,128]{4,3,2,1,0:T(2,128)} %subtract_bitcast_fusion) | data formatting | bytes 8388608 | tf_op jit(solution)/shard_map/reshape | solution.py:56
  220.0 18.4 %add_bitcast_fusion = f32[2,16,128,2,128]{4,3,2,1,0:T(2,128)} fusion(f32[2,16,128,128,2]{3,4,2,1,0:T(2,128)} %fusion.92, f32[2,16,128,128,2]{3,4,2,1,0:T(2,128)} %copy.82), kind=kOutput, calls=%fused_computation.6 | convolution fusion | flops 26214456 | bytes 12582912 | tf_op jit(solution)/shard_map/...a,ak->...k/dot_general | solution.py:25
  238.4 6.7 %reshape.227 = f32[2,16,128,256]{3,2,1,0:T(8,128)} reshape(f32[2,16,128,2,128]{4,3,2,1,0:T(2,128)} %add_bitcast_fusion) | data formatting | bytes 8388608 | tf_op jit(solution)/shard_map/reshape | solution.py:57
  245.1 6.5 %multiply_add_fusion.1 = (f32[1,16,256,128]{2,3,1,0:T(8,128)}, f32[1,16,256,128]{2,3,1,0:T(8,128)}) fusion(f32[2,16,256,128]{2,3,1,0:T(8,128)} %bitcast.198, f32[2,16,256,128]{2,3,1,0:T(8,128)} %bitcast.197), kind=kLoop, calls=%fused_computation.24 | loop fusion | flops 3145728 | bytes 12582912 | tf_op jit(solution)/shard_map/add | solution.py:82
  251.6 2.9 copy.85
  254.5 2.9 sub.70
  257.4 5.2 %fusion.31 = f32[128,16,256]{2,0,1:T(8,128)} fusion(f32[16,128,256]{2,1,0:T(8,128)} %sub.70), kind=kOutput, calls=%fused_computation.69 | convolution fusion | flops 805535744 | bytes 4194304 | tf_op jit(solution)/shard_map/...ab,ac->...cb/dot_general | solution.py:24
  262.6 3.5 fusion.45
  266.1 3.0 copy.86
  271.9 4.6 %convolution_add_fusion.2 = f32[128,16,256]{2,0,1:T(8,128)S(1)} fusion(f32[128,16,256]{2,0,1:T(8,128)} %fusion.31, f32[16,128,256]{2,1,0:T(8,128)} %add.212), kind=kOutput, calls=%fused_computation.33 | convolution fusion | flops 806060032 | bytes 6291456 | tf_op jit(solution)/shard_map/...ab,ac->...cb/dot_general | solution.py:25
  276.5 4.8 %add_bitcast_fusion.4 = (f32[16,128,256]{2,1,0:T(8,128)}, f32[16,128,256]{2,1,0:T(8,128)}) fusion(f32[128,16,256]{2,0,1:T(8,128)S(1)} %convolution_add_fusion.2, f32[128,256]{1,0:T(8,128)S(1)} %get-tuple-element.24, f32[128,256]{1,0:T(8,128)S(1)} %copy-done.18, f32[128,16,256]{2,0,1:T(8,128)S(1)} %copy-done.13, f32[16,128,256]{2,1,0:T(8,128)S(1)} %copy-done.6), kind=kOutput, calls=%fused_computation.22 | convolution fusion | flops 809205760 | bytes 10747904 | tf_op jit(solution)/shard_map/...ab,ac->...cb/dot_general | solution.py:23
  281.3 3.0 copy.87
  284.3 3.3 copy.88
  287.7 5.2 %fusion.28 = f32[128,16,128,2]{2,0,3,1:T(8,128)} fusion(f32[16,128,128,2]{2,1,3,0:T(8,128)} %copy.88), kind=kOutput, calls=%fused_computation.66 | convolution fusion | flops 805535744 | bytes 4194304 | tf_op jit(solution)/shard_map/...ab,ac->...cb/dot_general | solution.py:24
  292.9 3.4 fusion.26
  296.3 3.1 copy.89
  299.4 2.9 copy.90
  302.3 4.5 %convolution_add_fusion.1 = f32[128,16,128,2]{2,0,3,1:T(8,128)S(1)} fusion(f32[128,16,128,2]{2,0,3,1:T(8,128)} %fusion.28, f32[16,128,128,2]{2,1,3,0:T(8,128)} %copy.90), kind=kOutput, calls=%fused_computation.31 | convolution fusion | flops 806060032 | bytes 6291456 | tf_op jit(solution)/shard_map/...ab,ac->...cb/dot_general | solution.py:25
  306.9 4.8 %add_bitcast_fusion.3 = (f32[16,128,128,2]{1,2,3,0:T(8,128)}, f32[16,128,128,2]{1,2,3,0:T(8,128)}) fusion(f32[128,16,128,2]{2,0,3,1:T(8,128)S(1)} %convolution_add_fusion.1, f32[128,2]{0,1:T(2,128)S(1)} %get-tuple-element.26, f32[128,2]{0,1:T(2,128)S(1)} %get-tuple-element.27, f32[128,16,128,2]{2,0,3,1:T(8,128)S(1)} %copy-done.14, ...), kind=kOutput, calls=%fused_computation.20 | convolution fusion | flops 809205760 | bytes 10487808 | tf_op jit(solution)/shard_map/...ab,ac->...cb/dot_general | solution.py:23
  311.7 4.1 copy.93
  315.8 9.9 %fusion.87 = f32[16,128,128,2]{2,3,1,0:T(2,128)} fusion(f32[16,128,128,2]{2,3,1,0:T(2,128)} %copy.93), kind=kOutput, calls=%fused_computation.125 | convolution fusion | flops 12582968 | bytes 4194304 | tf_op jit(solution)/shard_map/...a,ak->...k/dot_general | solution.py:22
  325.7 4.1 copy.94
  329.8 10.2 %subtract_bitcast_fusion.3 = f32[16,128,2,128]{3,2,1,0:T(2,128)} fusion(f32[16,128,128,2]{2,3,1,0:T(2,128)} %fusion.87, f32[16,128,128,2]{2,3,1,0:T(2,128)} %copy.94), kind=kOutput, calls=%fused_computation.19 | convolution fusion | flops 13107256 | bytes 6291456 | tf_op jit(solution)/shard_map/...a,ak->...k/dot_general | solution.py:23
  340.0 4.1 copy.107
  347.2 31.6 %all_to_all.48 = f32[16,16,1024]{2,0,1:T(8,128)S(1)} all-to-all(f32[16,16,1024]{2,0,1:T(8,128)S(1)} %bitcast.217), channel_id=1, replica_groups=mesh['ctx'=16,'ch'=2] {'ctx'}, dimensions={1} | all-to-all | bytes 2097152 | tf_op jit(solution)/shard_map/all_to_all | solution.py:85
  379.8 21.8 %all-gather.2.cloned.1.call-done = bf16[512,1024]{1,0:T(8,128)(2,1)} async-done(((bf16[256,1024]{1,0:T(8,128)(2,1)}), bf16[512,1024]{1,0:T(8,128)(2,1)}) %all-gather.2.cloned.1.call-update) | async-done | bytes 1048592 | tf_op jit(solution)/shard_map/all_gather | solution.py:99
  401.7 5.6 %convolution_convert_fusion = bf16[1024,2048]{1,0:T(8,128)(2,1)} fusion(bf16[512,1024]{1,0:T(8,128)(2,1)} %all-gather.2.cloned.1.call-done, bf16[512,2048]{1,0:T(8,128)(2,1)S(1)} %copy-done), kind=kOutput, calls=%fused_computation.12 | convolution fusion | flops 2149580800 | bytes 7340032 | tf_op jit(solution)/shard_map/cb,cd->bd/dot_general | solution.py:101
  (69 shorter events, 32.2 us)
Async XLA Ops:
  6.5 395.1 %copy-start = (bf16[512,2048]{1,0:T(8,128)(2,1)S(1)}, bf16[512,2048]{1,0:T(8,128)(2,1)}, u32[]{:S(2)}) copy-start(bf16[512,2048]{1,0:T(8,128)(2,1)} %param.13) | copy-start | bytes 6291460
  6.5 12.8 %copy-start.16 = (bf16[256,1024]{1,0:T(8,128)(2,1)S(1)}, bf16[256,1024]{1,0:T(8,128)(2,1)}, u32[]{:S(2)}) copy-start(bf16[256,1024]{1,0:T(8,128)(2,1)} %param.8) | copy-start | bytes 1572868
  6.5 12.8 %copy-start.15 = (bf16[256,1024]{1,0:T(8,128)(2,1)S(1)}, bf16[256,1024]{1,0:T(8,128)(2,1)}, u32[]{:S(2)}) copy-start(bf16[256,1024]{1,0:T(8,128)(2,1)} %param.9) | copy-start | bytes 1572868
  6.5 11.7 %copy-start.19 = (bf16[3,256,3]{1,2,0:T(4,128)(2,1)S(1)}, bf16[3,256,3]{1,2,0:T(4,128)(2,1)}, u32[]{:S(2)}) copy-start(bf16[3,256,3]{1,2,0:T(4,128)(2,1)} %param.10) | copy-start | bytes 13828
  6.5 30.7 %all-to-all-start.1 = ((f32[16,16,1024]{2,1,0:T(8,128)}), f32[16,16,1024]{2,1,0:T(8,128)}, u32[]{:S(2)}, u32[]{:S(2)}) async-start(f32[16,16,1024]{2,1,0:T(8,128)} %bitcast.218), calls=%async_computation.1 | async-start | bytes 2097152 | tf_op jit(solution)/shard_map/all_to_all | solution.py:75
  14.3 5.1 %copy-start.17 = (bf16[256,1024]{1,0:T(8,128)(2,1)S(1)}, bf16[256,1024]{1,0:T(8,128)(2,1)}, u32[]{:S(2)}) copy-start(bf16[256,1024]{1,0:T(8,128)(2,1)} %param.7) | copy-start | bytes 1572868
  16.0 3.3 collective-permute-start
  22.4 1.6 copy-start.4
  37.2 37.3 %all-to-all-start = ((f32[16,16,1024]{2,1,0:T(8,128)}), f32[16,16,1024]{2,1,0:T(8,128)S(1)}, u32[]{:S(2)}, u32[]{:S(2)}) async-start(f32[16,16,1024]{2,1,0:T(8,128)} %bitcast.11), calls=%async_computation | async-start | bytes 2097152 | tf_op jit(solution)/shard_map/all_to_all | solution.py:74
  51.6 350.1 %all-gather.2.cloned.1.call-start = ((), (), s32[]{:S(2)}) async-start(), calls=%async_computation.3 | async-start | bytes 1572864 | tf_op jit(solution)/shard_map/all_gather | solution.py:99
  79.0 2.2 copy-start.10
  81.2 4.7 %copy-start.11 = (f32[128,2,16,256]{3,0,2,1:T(8,128)S(1)}, f32[128,2,16,256]{3,0,2,1:T(8,128)}, u32[]{:S(2)}) copy-start(f32[128,2,16,256]{3,0,2,1:T(8,128)} %fusion.10) | copy-start | bytes 12582916
  106.1 8.2 %copy-start.3 = (f32[2,16,128,128,2]{3,2,4,1,0:T(8,128)S(1)}, f32[2,16,128,128,2]{3,2,4,1,0:T(8,128)}, u32[]{:S(2)}) copy-start(f32[2,16,128,128,2]{3,2,4,1,0:T(8,128)} %copy.76) | copy-start | bytes 12582916
  130.9 7.8 %copy-start.2 = (f32[2,16,128,128,2]{3,2,4,1,0:T(8,128)S(1)}, f32[2,16,128,128,2]{3,2,4,1,0:T(8,128)}, u32[]{:S(2)}) copy-start(f32[2,16,128,128,2]{3,2,4,1,0:T(8,128)} %copy.78) | copy-start | bytes 12582916
  130.9 7.8 %copy-start.12 = (f32[128,2,16,128,2]{3,0,4,2,1:T(8,128)S(1)}, f32[128,2,16,128,2]{3,0,4,2,1:T(8,128)}, u32[]{:S(2)}) copy-start(f32[128,2,16,128,2]{3,0,4,2,1:T(8,128)} %fusion.35) | copy-start | bytes 12582916
  153.5 18.1 %copy-start.1 = (f32[2,16,128,128,2]{3,4,2,1,0:T(2,128)S(1)}, f32[2,16,128,128,2]{3,4,2,1,0:T(2,128)}, u32[]{:S(2)}) copy-start(f32[2,16,128,128,2]{3,4,2,1,0:T(2,128)} %copy.81) | copy-start | bytes 12582916
  257.4 5.2 %copy-start.8 = (f32[16,128,256]{2,1,0:T(8,128)S(1)}, f32[16,128,256]{2,1,0:T(8,128)}, u32[]{:S(2)}) copy-start(f32[16,128,256]{2,1,0:T(8,128)} %sub.70) | copy-start | bytes 6291460
  271.9 4.6 %copy-start.6 = (f32[16,128,256]{2,1,0:T(8,128)S(1)}, f32[16,128,256]{2,1,0:T(8,128)}, u32[]{:S(2)}) copy-start(f32[16,128,256]{2,1,0:T(8,128)} %add.212) | copy-start | bytes 6291460
  271.9 4.6 %copy-start.13 = (f32[128,16,256]{2,0,1:T(8,128)S(1)}, f32[128,16,256]{2,0,1:T(8,128)}, u32[]{:S(2)}) copy-start(f32[128,16,256]{2,0,1:T(8,128)} %fusion.45) | copy-start | bytes 6291460
  271.9 4.6 %copy-start.18 = (f32[128,256]{1,0:T(8,128)S(1)}, f32[128,256]{1,0:T(8,128)}, u32[]{:S(2)}) copy-start(f32[128,256]{1,0:T(8,128)} %get-tuple-element.25) | copy-start | bytes 393220
  287.7 5.2 %copy-start.9 = (f32[16,128,128,2]{2,1,3,0:T(8,128)S(1)}, f32[16,128,128,2]{2,1,3,0:T(8,128)}, u32[]{:S(2)}) copy-start(f32[16,128,128,2]{2,1,3,0:T(8,128)} %copy.88) | copy-start | bytes 6291460
  302.3 4.5 %copy-start.7 = (f32[16,128,128,2]{2,1,3,0:T(8,128)S(1)}, f32[16,128,128,2]{2,1,3,0:T(8,128)}, u32[]{:S(2)}) copy-start(f32[16,128,128,2]{2,1,3,0:T(8,128)} %copy.90) | copy-start | bytes 6291460
  302.3 4.6 %copy-start.14 = (f32[128,16,128,2]{2,0,3,1:T(8,128)S(1)}, f32[128,16,128,2]{2,0,3,1:T(8,128)}, u32[]{:S(2)}) copy-start(f32[128,16,128,2]{2,0,3,1:T(8,128)} %fusion.26) | copy-start | bytes 6291460
  346.9 31.8 %copy-start.5 = (f32[3,256,1024]{2,1,0:T(8,128)S(1)}, f32[3,256,1024]{2,1,0:T(8,128)}, u32[]{:S(2)}) copy-start(f32[3,256,1024]{2,1,0:T(8,128)} %copy-done.4) | copy-start | bytes 9437188
  347.0 31.8 %copy-start.20 = (f32[256]{0:T(256)S(1)}, f32[256]{0:T(256)}, u32[]{:S(2)}) copy-start(f32[256]{0:T(256)} %param.12) | copy-start | bytes 3076
Sparse Core Ops, SparseCore 0:
  380.0 21.6 all-gather.1
where the time goes:
time: 419 us; the launch traced here: 414 us
  matrix products  184 us (44%)
  local copies, waits for them, and re-layouts  101 us (24%)
  waiting for transfers between devices  42.5 us (10%)
  blocking collectives  31.6 us (8%)
  starting transfers between devices  25 us (6%)
  other arithmetic  16.7 us (4%)
  between operations  13.9 us (3%)
    dot_general x6, matrix products, complex_contract(): imag_imag = jnp.einsum(pattern, left_imag, right_imag, precision=exact_mode)  49.7 us
    dot_general x6, matrix products, complex_contract(): real_real = jnp.einsum(pattern, left_real, right_real, precision=exact_mode)  45.3 us
    dot_general x5, matrix products, complex_contract(): real_imag = jnp.einsum(pattern, left_real, right_imag, precision=exact_mode)  44.1 us
    dot_general x5, matrix products, complex_contract(): imag_real = jnp.einsum(pattern, left_imag, right_real, precision=exact_mode)  39.1 us
    all_to_all x1, blocking collectives, long_by_channel(): lax.all_to_all(result_rows, 'ctx', split_axis=1, concat_axis=0, tiled=True)  31.6 us
    all_gather x1, waiting for transfers between devices, local(): lax.all_gather(part, 'ch', axis=0, tiled=True)  21.8 us
    add x4, local copies, waits for them, and re-layouts, transform_last(): section_real * twist_sin + section_imag * twist_cos  20.1 us
    sub x4, local copies, waits for them, and re-layouts, transform_last(): section_real * twist_cos - section_imag * twist_sin  19.8 us
  transfers between devices with their start and end apart: 4, of which 4 were waited for; matrix products, arithmetic and copies ran while one was open for 5% of the time, Pallas kernels for 0%

commit v1 on v0

--- a/solution.py
+++ b/solution.py
@@ -5,6 +5,27 @@
 from jax.sharding import PartitionSpec as P
 
 exact_mode = lax.Precision.HIGHEST
+
+
+def laid_out(parts, dim):
+    shape = list(parts.shape[1:])
+    shape[dim] *= parts.shape[0]
+    return jnp.moveaxis(parts, 0, dim).reshape(shape)
+
+
+def doubled(x, axis):
+    size, here = (lax.axis_size(axis), lax.axis_index(axis))
+    pieces, apart = (x[None], 1)
+    while apart < size:
+        theirs = lax.ppermute(pieces, axis, [(i, i ^ apart) for i in range(size)])
+        low = here & apart == 0
+        pieces = jnp.concatenate([jnp.where(low, pieces, theirs), jnp.where(low, theirs, pieces)])
+        apart *= 2
+    return pieces
+
+
+def collect(shard, axis, dim):
+    return laid_out(doubled(shard, axis), dim)
 
 
 def passed_along(value, axis, steps):
@@ -96,7 +117,7 @@
     long_out = long_by_channel(product_kv, long_filter)
     gated_rows = (query_short * (long_out + skip_gain[:, None] * product_kv)).astype(jnp.bfloat16)
     initial = jnp.zeros((tokens, out_weight.shape[1]), jnp.float32)
-    piece = jax.tree.map(lambda part: lax.all_gather(part, "ch", axis=0, tiled=True), gated_rows)
+    piece = jax.tree.map(lambda part: collect(part, "ch", 0), gated_rows)
     weight_rows = lax.slice_in_dim(out_weight, 0, piece.shape[0], axis=0)
     summed = initial + jnp.einsum(
         "cb,cd->bd", piece, weight_rows, preferred_element_type=jnp.float32

time: 419 us -> 397 us (0.947)
  between operations: 13.9 us -> 0.54 us
  waiting for transfers between devices: 42.5 us -> 34.5 us
    all_gather x1 -> x0, waiting for transfers between devices: 21.8 us -> none  [local(): lax.all_gather(part, 'ch', axis=0, tiled=True)]
    ppermute x0 -> x1, waiting for transfers between devices: none -> 13.3 us  [doubled(): theirs = lax.ppermute(pieces, axis, [(i, i ^ apart) for i in range(size)])]
where the time goes in v1:
time: 397 us; the launch traced here: 393 us
  matrix products  182 us (46%)
  local copies, waits for them, and re-layouts  101 us (25%)
  waiting for transfers between devices  34.5 us (9%)
  blocking collectives  31.6 us (8%)
  starting transfers between devices  26.6 us (7%)
  other arithmetic  16.1 us (4%)
    dot_general x6, matrix products, complex_contract(): imag_imag = jnp.einsum(pattern, left_imag, right_imag, precision=exact_mode)  49.7 us
    dot_general x6, matrix products, complex_contract(): real_real = jnp.einsum(pattern, left_real, right_real, precision=exact_mode)  45.3 us
    dot_general x5, matrix products, complex_contract(): real_imag = jnp.einsum(pattern, left_real, right_imag, precision=exact_mode)  44.1 us
    dot_general x5, matrix products, complex_contract(): imag_real = jnp.einsum(pattern, left_imag, right_real, precision=exact_mode)  39.1 us
    all_to_all x1, blocking collectives, long_by_channel(): lax.all_to_all(result_rows, 'ctx', split_axis=1, concat_axis=0, tiled=True)  31.6 us
    add x4, local copies, waits for them, and re-layouts, transform_last(): section_real * twist_sin + section_imag * twist_cos  20 us
    sub x4, local copies, waits for them, and re-layouts, transform_last(): section_real * twist_cos - section_imag * twist_sin  19.9 us
    all_to_all x1, starting transfers between devices, long_by_channel(): lax.all_to_all(signal, 'ctx', split_axis=0, concat_axis=1, tiled=True)  15 us
  transfers between devices with their start and end apart: 4, of which 4 were waited for; matrix products, arithmetic and copies ran while one was open for 5% of the time, Pallas kernels for 0%

profile of v1, /device:TPU:0, one launch (start us, length us, event | category | flops | bytes accessed | tf_op | source)
XLA Modules:
  0.0 392.7 jit_solution(12104842126940250411)
XLA Ops:
  0.0 7.7 %all-to-all-start.1 = ((f32[16,16,1024]{2,1,0:T(8,128)}), f32[16,16,1024]{2,1,0:T(8,128)}, u32[]{:S(2)}, u32[]{:S(2)}) async-start(f32[16,16,1024]{2,1,0:T(8,128)} %bitcast.209), calls=%async_computation.1 | async-start | bytes 2097152 | tf_op jit(solution)/shard_map/all_to_all | solution.py:96
  18.7 12.0 %all-to-all-done.1 = f32[16,16,1024]{2,1,0:T(8,128)} async-done(((f32[16,16,1024]{2,1,0:T(8,128)}), f32[16,16,1024]{2,1,0:T(8,128)}, u32[]{:S(2)}, u32[]{:S(2)}) %all-to-all-start.1) | async-done | bytes 1048608 | tf_op jit(solution)/shard_map/all_to_all | solution.py:96
  30.7 15.0 %all-to-all-start = ((f32[16,16,1024]{2,1,0:T(8,128)}), f32[16,16,1024]{2,1,0:T(8,128)S(1)}, u32[]{:S(2)}, u32[]{:S(2)}) async-start(f32[16,16,1024]{2,1,0:T(8,128)} %bitcast.10), calls=%async_computation | async-start | bytes 2097152 | tf_op jit(solution)/shard_map/all_to_all | solution.py:95
  47.5 3.8 fusion.12
  51.3 3.8 fusion.10
  60.3 8.3 %all-to-all-done = f32[16,16,1024]{2,1,0:T(8,128)S(1)} async-done(((f32[16,16,1024]{2,1,0:T(8,128)}), f32[16,16,1024]{2,1,0:T(8,128)S(1)}, u32[]{:S(2)}, u32[]{:S(2)}) %all-to-all-start) | async-done | bytes 1048608 | tf_op jit(solution)/shard_map/all_to_all | solution.py:95
  75.3 4.7 %fusion.4 = f32[128,2,16,256]{3,0,2,1:T(8,128)S(1)} fusion(f32[128,2,16,256]{3,0,2,1:T(8,128)S(1)} %copy-done.10, f32[2,16,128,256]{3,2,1,0:T(8,128)S(1)} %bitcast.186), kind=kOutput, calls=%fused_computation.14 | convolution fusion | flops 1611890688 | bytes 12582912 | tf_op jit(solution)/shard_map/...ab,ac->...cb/dot_general | solution.py:43
  80.0 9.3 %add_bitcast_fusion.2 = (f32[2,16,128,256]{3,2,1,0:T(8,128)}, f32[2,16,128,256]{3,2,1,0:T(8,128)}) fusion(f32[128,2,16,256]{3,0,2,1:T(8,128)S(1)} %fusion.4, f32[128,256]{1,0:T(8,128)S(1)} %get-tuple-element.22, f32[128,256]{1,0:T(8,128)S(1)} %get-tuple-element.23, f32[128,2,16,256]{3,0,2,1:T(8,128)S(1)} %copy-done.11, f32[2,16,128,256]{3,2,1,0:T(8,128)S(1)} %bitcast.187), kind=kOutput, calls=%fused_computation.10 | convolution fusion | flops 1618182144 | bytes 21233664 | tf_op jit(solution)/shard_map/...ab,ac->...cb/dot_general | solution.py:45
  89.2 5.4 %copy.75 = f32[2,16,128,256]{2,1,3,0:T(8,128)} copy(f32[2,16,128,256]{3,2,1,0:T(8,128)} %get-tuple-element.6) | data formatting | bytes 8388608 | tf_op jit(solution)/shard_map/sub | solution.py:72
  94.7 5.4 %copy.76 = f32[2,16,128,128,2]{3,2,4,1,0:T(8,128)} copy(f32[2,16,128,128,2]{2,1,4,3,0:T(8,128)} %bitcast.191) | data formatting | bytes 8388608 | tf_op jit(solution)/shard_map/reshape | solution.py:65
  100.1 8.2 %fusion.36 = f32[128,2,16,128,2]{3,0,4,2,1:T(8,128)} fusion(f32[2,16,128,128,2]{3,2,4,1,0:T(8,128)} %copy.76), kind=kOutput, calls=%fused_computation.76 | convolution fusion | flops 1610842112 | bytes 8388608 | tf_op jit(solution)/shard_map/...ab,ac->...cb/dot_general | solution.py:45
  108.3 5.6 %fusion.34 = f32[128,2,16,128,2]{3,0,4,2,1:T(8,128)} fusion(f32[2,16,128,128,2]{3,2,4,1,0:T(8,128)S(1)} %copy-done.3), kind=kOutput, calls=%fused_computation.74 | convolution fusion | flops 1610842112 | bytes 8388608 | tf_op jit(solution)/shard_map/...ab,ac->...cb/dot_general | solution.py:43
  113.9 5.7 %copy.77 = f32[2,16,128,256]{2,1,3,0:T(8,128)} copy(f32[2,16,128,256]{3,2,1,0:T(8,128)} %get-tuple-element.5) | data formatting | bytes 8388608 | tf_op jit(solution)/shard_map/add | solution.py:73
  119.6 5.3 %copy.78 = f32[2,16,128,128,2]{3,2,4,1,0:T(8,128)} copy(f32[2,16,128,128,2]{2,1,4,3,0:T(8,128)} %bitcast.192) | data formatting | bytes 8388608 | tf_op jit(solution)/shard_map/reshape | solution.py:66
  124.9 7.8 %convolution_add_fusion = f32[128,2,16,128,2]{3,0,4,2,1:T(8,128)S(1)} fusion(f32[128,2,16,128,2]{3,0,4,2,1:T(8,128)} %fusion.36, f32[2,16,128,128,2]{3,2,4,1,0:T(8,128)} %copy.78), kind=kOutput, calls=%fused_computation.16 | convolution fusion | flops 1611890688 | bytes 12582912 | tf_op jit(solution)/shard_map/...ab,ac->...cb/dot_general | solution.py:46
  132.7 7.6 %add_bitcast_fusion.1 = (f32[2,16,128,128,2]{2,3,4,1,0:T(8,128)}, f32[2,16,128,128,2]{2,3,4,1,0:T(8,128)}) fusion(f32[128,2,16,128,2]{3,0,4,2,1:T(8,128)S(1)} %convolution_add_fusion, f32[128,2]{0,1:T(2,128)S(1)} %get-tuple-element.24, f32[128,2]{0,1:T(2,128)S(1)} %get-tuple-element.25, f32[128,2,16,128,2]{3,0,4,2,1:T(8,128)S(1)} %copy-done.12, ...), kind=kOutput, calls=%fused_computation.8 | convolution fusion | flops 1618182144 | bytes 20973568 | tf_op jit(solution)/shard_map/...ab,ac->...cb/dot_general | solution.py:44
  140.2 7.2 %copy.81 = f32[2,16,128,128,2]{3,4,2,1,0:T(2,128)} copy(f32[2,16,128,128,2]{2,3,4,1,0:T(8,128)} %get-tuple-element.8) | data formatting | bytes 8388608 | tf_op jit(solution)/shard_map/sub | solution.py:72
  147.5 18.2 %fusion.89 = f32[2,16,128,128,2]{3,4,2,1,0:T(2,128)} fusion(f32[2,16,128,128,2]{3,4,2,1,0:T(2,128)} %copy.81), kind=kOutput, calls=%fused_computation.129 | convolution fusion | flops 25165880 | bytes 8388608 | tf_op jit(solution)/shard_map/...a,ak->...k/dot_general | solution.py:43
  165.7 16.2 %fusion.91 = f32[2,16,128,128,2]{3,4,2,1,0:T(2,128)} fusion(f32[2,16,128,128,2]{3,4,2,1,0:T(2,128)S(1)} %copy-done.1), kind=kOutput, calls=%fused_computation.131 | convolution fusion | flops 25165880 | bytes 8388608 | tf_op jit(solution)/shard_map/...a,ak->...k/dot_general | solution.py:45
  181.9 7.2 %copy.82 = f32[2,16,128,128,2]{3,4,2,1,0:T(2,128)} copy(f32[2,16,128,128,2]{2,3,4,1,0:T(8,128)} %get-tuple-element.7) | data formatting | bytes 8388608 | tf_op jit(solution)/shard_map/add | solution.py:73
  189.1 18.5 %subtract_bitcast_fusion = f32[2,16,128,2,128]{4,3,2,1,0:T(2,128)} fusion(f32[2,16,128,128,2]{3,4,2,1,0:T(2,128)} %fusion.89, f32[2,16,128,128,2]{3,4,2,1,0:T(2,128)} %copy.82), kind=kOutput, calls=%fused_computation.7 | convolution fusion | flops 26214456 | bytes 12582912 | tf_op jit(solution)/shard_map/...a,ak->...k/dot_general | solution.py:44
  207.6 6.4 %reshape.231 = f32[2,16,128,256]{3,2,1,0:T(8,128)} reshape(f32[2,16,128,2,128]{4,3,2,1,0:T(2,128)} %subtract_bitcast_fusion) | data formatting | bytes 8388608 | tf_op jit(solution)/shard_map/reshape | solution.py:77
  214.0 18.4 %add_bitcast_fusion = f32[2,16,128,2,128]{4,3,2,1,0:T(2,128)} fusion(f32[2,16,128,128,2]{3,4,2,1,0:T(2,128)} %fusion.91, f32[2,16,128,128,2]{3,4,2,1,0:T(2,128)} %copy.82), kind=kOutput, calls=%fused_computation.6 | convolution fusion | flops 26214456 | bytes 12582912 | tf_op jit(solution)/shard_map/...a,ak->...k/dot_general | solution.py:46
  232.4 6.7 %reshape.232 = f32[2,16,128,256]{3,2,1,0:T(8,128)} reshape(f32[2,16,128,2,128]{4,3,2,1,0:T(2,128)} %add_bitcast_fusion) | data formatting | bytes 8388608 | tf_op jit(solution)/shard_map/reshape | solution.py:78
  239.1 6.5 %multiply_add_fusion.1 = (f32[1,16,256,128]{2,3,1,0:T(8,128)}, f32[1,16,256,128]{2,3,1,0:T(8,128)}) fusion(f32[2,16,256,128]{2,3,1,0:T(8,128)} %bitcast.189, f32[2,16,256,128]{2,3,1,0:T(8,128)} %bitcast.188), kind=kLoop, calls=%fused_computation.24 | loop fusion | flops 3145728 | bytes 12582912 | tf_op jit(solution)/shard_map/add | solution.py:103
  245.6 2.9 copy.85
  248.5 2.9 sub.70
  251.4 5.2 %fusion.30 = f32[128,16,256]{2,0,1:T(8,128)} fusion(f32[16,128,256]{2,1,0:T(8,128)} %sub.70), kind=kOutput, calls=%fused_computation.70 | convolution fusion | flops 805535744 | bytes 4194304 | tf_op jit(solution)/shard_map/...ab,ac->...cb/dot_general | solution.py:45
  256.6 3.5 fusion.44
  260.1 2.9 copy.86
  265.9 4.6 %convolution_add_fusion.2 = f32[128,16,256]{2,0,1:T(8,128)S(1)} fusion(f32[128,16,256]{2,0,1:T(8,128)} %fusion.30, f32[16,128,256]{2,1,0:T(8,128)} %add.213), kind=kOutput, calls=%fused_computation.33 | convolution fusion | flops 806060032 | bytes 6291456 | tf_op jit(solution)/shard_map/...ab,ac->...cb/dot_general | solution.py:46
  270.5 4.8 %add_bitcast_fusion.4 = (f32[16,128,256]{2,1,0:T(8,128)}, f32[16,128,256]{2,1,0:T(8,128)}) fusion(f32[128,16,256]{2,0,1:T(8,128)S(1)} %convolution_add_fusion.2, f32[128,256]{1,0:T(8,128)S(1)} %get-tuple-element.26, f32[128,256]{1,0:T(8,128)S(1)} %copy-done.18, f32[128,16,256]{2,0,1:T(8,128)S(1)} %copy-done.13, f32[16,128,256]{2,1,0:T(8,128)S(1)} %copy-done.6), kind=kOutput, calls=%fused_computation.22 | convolution fusion | flops 809205760 | bytes 10747904 | tf_op jit(solution)/shard_map/...ab,ac->...cb/dot_general | solution.py:44
  275.3 3.0 copy.87
  278.3 3.3 copy.88
  281.6 5.2 %fusion.27 = f32[128,16,128,2]{2,0,3,1:T(8,128)} fusion(f32[16,128,128,2]{2,1,3,0:T(8,128)} %copy.88), kind=kOutput, calls=%fused_computation.67 | convolution fusion | flops 805535744 | bytes 4194304 | tf_op jit(solution)/shard_map/...ab,ac->...cb/dot_general | solution.py:45
  286.9 3.5 fusion.25
  290.3 3.1 copy.89
  293.4 2.9 copy.90
  296.3 4.5 %convolution_add_fusion.1 = f32[128,16,128,2]{2,0,3,1:T(8,128)S(1)} fusion(f32[128,16,128,2]{2,0,3,1:T(8,128)} %fusion.27, f32[16,128,128,2]{2,1,3,0:T(8,128)} %copy.90), kind=kOutput, calls=%fused_computation.31 | convolution fusion | flops 806060032 | bytes 6291456 | tf_op jit(solution)/shard_map/...ab,ac->...cb/dot_general | solution.py:46
  300.9 4.8 %add_bitcast_fusion.3 = (f32[16,128,128,2]{1,2,3,0:T(8,128)}, f32[16,128,128,2]{1,2,3,0:T(8,128)}) fusion(f32[128,16,128,2]{2,0,3,1:T(8,128)S(1)} %convolution_add_fusion.1, f32[128,2]{0,1:T(2,128)S(1)} %get-tuple-element.28, f32[128,2]{0,1:T(2,128)S(1)} %get-tuple-element.29, f32[128,16,128,2]{2,0,3,1:T(8,128)S(1)} %copy-done.14, ...), kind=kOutput, calls=%fused_computation.20 | convolution fusion | flops 809205760 | bytes 10487808 | tf_op jit(solution)/shard_map/...ab,ac->...cb/dot_general | solution.py:44
  305.7 4.1 %copy.93 = f32[16,128,128,2]{2,3,1,0:T(2,128)} copy(f32[16,128,128,2]{1,2,3,0:T(8,128)} %get-tuple-element.14) | data formatting | bytes 4194304 | tf_op jit(solution)/shard_map/sub | solution.py:72
  309.8 9.9 %fusion.86 = f32[16,128,128,2]{2,3,1,0:T(2,128)} fusion(f32[16,128,128,2]{2,3,1,0:T(2,128)} %copy.93), kind=kOutput, calls=%fused_computation.126 | convolution fusion | flops 12582968 | bytes 4194304 | tf_op jit(solution)/shard_map/...a,ak->...k/dot_general | solution.py:43
  319.7 4.1 %copy.94 = f32[16,128,128,2]{2,3,1,0:T(2,128)} copy(f32[16,128,128,2]{1,2,3,0:T(8,128)} %get-tuple-element.13) | data formatting | bytes 4194304 | tf_op jit(solution)/shard_map/add | solution.py:73
  323.8 10.2 %subtract_bitcast_fusion.3 = f32[16,128,2,128]{3,2,1,0:T(2,128)} fusion(f32[16,128,128,2]{2,3,1,0:T(2,128)} %fusion.86, f32[16,128,128,2]{2,3,1,0:T(2,128)} %copy.94), kind=kOutput, calls=%fused_computation.19 | convolution fusion | flops 13107256 | bytes 6291456 | tf_op jit(solution)/shard_map/...a,ak->...k/dot_general | solution.py:44
  334.0 4.1 %copy.107 = f32[16,128,2,128]{1,3,2,0:T(8,128)} copy(f32[16,128,2,128]{3,2,1,0:T(2,128)} %subtract_bitcast_fusion.3) | data formatting | bytes 4194304 | tf_op jit(solution)/shard_map/reshape | solution.py:77
  341.1 31.6 %all_to_all.48 = f32[16,16,1024]{2,0,1:T(8,128)S(1)} all-to-all(f32[16,16,1024]{2,0,1:T(8,128)S(1)} %bitcast.208), channel_id=1, replica_groups=mesh['ctx'=16,'ch'=2] {'ctx'}, dimensions={1} | all-to-all | bytes 2097152 | tf_op jit(solution)/shard_map/all_to_all | solution.py:106
  374.6 13.3 %collective-permute-done.1 = bf16[1,256,1024]{2,1,0:T(8,128)(2,1)S(1)} collective-permute-done((bf16[1,256,1024]{2,1,0:T(8,128)(2,1)S(1)}, bf16[1,256,1024]{2,1,0:T(8,128)(2,1)S(1)}, u32[]{:S(2)}, u32[]{:S(2)}) %collective-permute-start.1) | collective-permute-done | bytes 524320 | tf_op jit(solution)/shard_map/ppermute | solution.py:20
  388.1 4.4 %convolution_convert_fusion = bf16[1024,2048]{1,0:T(8,128)(2,1)} fusion(bf16[512,1024]{1,0:T(8,128)(2,1)S(1)} %bitcast.210, bf16[512,2048]{1,0:T(8,128)(2,1)S(1)} %copy-done), kind=kOutput, calls=%fused_computation.12 | convolution fusion | flops 2149580800 | bytes 7340032 | tf_op jit(solution)/shard_map/cb,cd->bd/dot_general | solution.py:122
  (70 shorter events, 32.5 us)
Async XLA Ops:
  0.0 388.1 %copy-start = (bf16[512,2048]{1,0:T(8,128)(2,1)S(1)}, bf16[512,2048]{1,0:T(8,128)(2,1)}, u32[]{:S(2)}) copy-start(bf16[512,2048]{1,0:T(8,128)(2,1)} %param.13) | copy-start | bytes 6291460
  0.0 12.8 %copy-start.16 = (bf16[256,1024]{1,0:T(8,128)(2,1)S(1)}, bf16[256,1024]{1,0:T(8,128)(2,1)}, u32[]{:S(2)}) copy-start(bf16[256,1024]{1,0:T(8,128)(2,1)} %param.8) | copy-start | bytes 1572868
  0.0 12.8 %copy-start.15 = (bf16[256,1024]{1,0:T(8,128)(2,1)S(1)}, bf16[256,1024]{1,0:T(8,128)(2,1)}, u32[]{:S(2)}) copy-start(bf16[256,1024]{1,0:T(8,128)(2,1)} %param.9) | copy-start | bytes 1572868
  0.0 11.7 %copy-start.19 = (bf16[3,256,3]{1,2,0:T(4,128)(2,1)S(1)}, bf16[3,256,3]{1,2,0:T(4,128)(2,1)}, u32[]{:S(2)}) copy-start(bf16[3,256,3]{1,2,0:T(4,128)(2,1)} %param.10) | copy-start | bytes 13828
  0.0 30.7 %all-to-all-start.1 = ((f32[16,16,1024]{2,1,0:T(8,128)}), f32[16,16,1024]{2,1,0:T(8,128)}, u32[]{:S(2)}, u32[]{:S(2)}) async-start(f32[16,16,1024]{2,1,0:T(8,128)} %bitcast.209), calls=%async_computation.1 | async-start | bytes 2097152 | tf_op jit(solution)/shard_map/all_to_all | solution.py:96
  7.7 5.1 %copy-start.17 = (bf16[256,1024]{1,0:T(8,128)(2,1)S(1)}, bf16[256,1024]{1,0:T(8,128)(2,1)}, u32[]{:S(2)}) copy-start(bf16[256,1024]{1,0:T(8,128)(2,1)} %param.7) | copy-start | bytes 1572868
  9.5 3.3 collective-permute-start
  15.9 1.6 copy-start.4
  30.7 37.9 %all-to-all-start = ((f32[16,16,1024]{2,1,0:T(8,128)}), f32[16,16,1024]{2,1,0:T(8,128)S(1)}, u32[]{:S(2)}, u32[]{:S(2)}) async-start(f32[16,16,1024]{2,1,0:T(8,128)} %bitcast.10), calls=%async_computation | async-start | bytes 2097152 | tf_op jit(solution)/shard_map/all_to_all | solution.py:95
  73.1 2.2 copy-start.10
  75.3 4.7 %copy-start.11 = (f32[128,2,16,256]{3,0,2,1:T(8,128)S(1)}, f32[128,2,16,256]{3,0,2,1:T(8,128)}, u32[]{:S(2)}) copy-start(f32[128,2,16,256]{3,0,2,1:T(8,128)} %fusion.10) | copy-start | bytes 12582916
  100.1 8.2 %copy-start.3 = (f32[2,16,128,128,2]{3,2,4,1,0:T(8,128)S(1)}, f32[2,16,128,128,2]{3,2,4,1,0:T(8,128)}, u32[]{:S(2)}) copy-start(f32[2,16,128,128,2]{3,2,4,1,0:T(8,128)} %copy.76) | copy-start | bytes 12582916
  124.9 7.8 %copy-start.2 = (f32[2,16,128,128,2]{3,2,4,1,0:T(8,128)S(1)}, f32[2,16,128,128,2]{3,2,4,1,0:T(8,128)}, u32[]{:S(2)}) copy-start(f32[2,16,128,128,2]{3,2,4,1,0:T(8,128)} %copy.78) | copy-start | bytes 12582916
  124.9 7.8 %copy-start.12 = (f32[128,2,16,128,2]{3,0,4,2,1:T(8,128)S(1)}, f32[128,2,16,128,2]{3,0,4,2,1:T(8,128)}, u32[]{:S(2)}) copy-start(f32[128,2,16,128,2]{3,0,4,2,1:T(8,128)} %fusion.34) | copy-start | bytes 12582916
  147.5 18.2 %copy-start.1 = (f32[2,16,128,128,2]{3,4,2,1,0:T(2,128)S(1)}, f32[2,16,128,128,2]{3,4,2,1,0:T(2,128)}, u32[]{:S(2)}) copy-start(f32[2,16,128,128,2]{3,4,2,1,0:T(2,128)} %copy.81) | copy-start | bytes 12582916
  251.4 5.2 %copy-start.8 = (f32[16,128,256]{2,1,0:T(8,128)S(1)}, f32[16,128,256]{2,1,0:T(8,128)}, u32[]{:S(2)}) copy-start(f32[16,128,256]{2,1,0:T(8,128)} %sub.70) | copy-start | bytes 6291460
  265.9 4.6 %copy-start.6 = (f32[16,128,256]{2,1,0:T(8,128)S(1)}, f32[16,128,256]{2,1,0:T(8,128)}, u32[]{:S(2)}) copy-start(f32[16,128,256]{2,1,0:T(8,128)} %add.213) | copy-start | bytes 6291460
  265.9 4.6 %copy-start.13 = (f32[128,16,256]{2,0,1:T(8,128)S(1)}, f32[128,16,256]{2,0,1:T(8,128)}, u32[]{:S(2)}) copy-start(f32[128,16,256]{2,0,1:T(8,128)} %fusion.44) | copy-start | bytes 6291460
  265.9 4.6 %copy-start.18 = (f32[128,256]{1,0:T(8,128)S(1)}, f32[128,256]{1,0:T(8,128)}, u32[]{:S(2)}) copy-start(f32[128,256]{1,0:T(8,128)} %get-tuple-element.27) | copy-start | bytes 393220
  281.6 5.2 %copy-start.9 = (f32[16,128,128,2]{2,1,3,0:T(8,128)S(1)}, f32[16,128,128,2]{2,1,3,0:T(8,128)}, u32[]{:S(2)}) copy-start(f32[16,128,128,2]{2,1,3,0:T(8,128)} %copy.88) | copy-start | bytes 6291460
  296.3 4.5 %copy-start.7 = (f32[16,128,128,2]{2,1,3,0:T(8,128)S(1)}, f32[16,128,128,2]{2,1,3,0:T(8,128)}, u32[]{:S(2)}) copy-start(f32[16,128,128,2]{2,1,3,0:T(8,128)} %copy.90) | copy-start | bytes 6291460
  296.3 4.6 %copy-start.14 = (f32[128,16,128,2]{2,0,3,1:T(8,128)S(1)}, f32[128,16,128,2]{2,0,3,1:T(8,128)}, u32[]{:S(2)}) copy-start(f32[128,16,128,2]{2,0,3,1:T(8,128)} %fusion.25) | copy-start | bytes 6291460
  340.9 31.8 %copy-start.5 = (f32[3,256,1024]{2,1,0:T(8,128)S(1)}, f32[3,256,1024]{2,1,0:T(8,128)}, u32[]{:S(2)}) copy-start(f32[3,256,1024]{2,1,0:T(8,128)} %copy-done.4) | copy-start | bytes 9437188
  340.9 31.8 %copy-start.20 = (f32[256]{0:T(256)S(1)}, f32[256]{0:T(256)}, u32[]{:S(2)}) copy-start(f32[256]{0:T(256)} %param.12) | copy-start | bytes 3076
  373.0 14.9 %collective-permute-start.1 = (bf16[1,256,1024]{2,1,0:T(8,128)(2,1)S(1)}, bf16[1,256,1024]{2,1,0:T(8,128)(2,1)S(1)}, u32[]{:S(2)}, u32[]{:S(2)}) collective-permute-start(bf16[1,256,1024]{2,1,0:T(8,128)(2,1)S(1)} %fusion.15), channel_id=1, source_target_pairs={{0,1},{1,0},{2,3},{3,2},{4,5},{5,4},{6,7},{7,6},{8,9},{9,8},{10,11... | collective-permute-start | bytes 1572872 | tf_op jit(solution)/shard_map/ppermute | solution.py:20
